TPU v7x, 256 devices: a whole 4x4x8 slice. The times are simulated.
256 devices in a mesh: row: 16 (over y, z_lo), col: 16 (over z_hi, x, core).
Axes of the slice: x: 4, y: 4, z: 8 (z_hi: 2, z_lo: 4; z = z_hi * 4 + z_lo), core: 2. Of those that a mesh axis runs over, the one named last changes fastest.
Arguments:
- start_vectors: float32 [64, 32768], P(None, ('row', 'col')), may hold values from -6 to 6
- cluster_order: int32 [256, 128], P(('row', 'col')), may hold values from 0 to 127, each once within a row
- weights: bfloat16 [32768, 16, 2048], P('row', 'col'), may hold values from 0 to 1, as said below
- block_mask: int32 [256, 16, 16], P('row', 'col'), may hold values 0 or 1
Outputs:
- embedding: float32 [64, 32768], P(None, ('row', 'col'))
Inputs may be any that keep to these rules, and one draw needn't show every extreme that they name: Each row of cluster_order holds every number of 0 to 127 once. `block_mask`: entries below the diagonal blocks are read only through their mirror. `weights`: every node except the last of its cluster block has a positive weight to the next node of its cluster block.
All inputs are finite; a program needn't handle non-finite values.
Results may differ from a plain program's by a relative error of at most 0.00087.
Values may be sent and summed in bfloat16 or wider, within the bound.
A program may use at most 64 MiB of HBM per device.

v0:
```python
import math
import jax
import jax.numpy as jnp
from jax import lax
from jax.sharding import PartitionSpec as P

ITERS = 3


def orthonormalize(panel_in):
    partial_gram = lax.dot_general(
        panel_in,
        panel_in,
        (((1,), (1,)), ((), ())),
        precision=lax.Precision.HIGHEST,
        preferred_element_type=jnp.float32,
    )
    total_gram = lax.psum(partial_gram, ("row", "col"))
    factor = jnp.linalg.cholesky(total_gram)
    return jax.scipy.linalg.solve_triangular(factor, panel_in, lower=True)


def collect_direct(term):
    return lax.psum_scatter(term, "col", scatter_dimension=1, tiled=True)


def direct_part(matrix, vectors):
    return lax.dot_general(
        lax.all_gather(vectors, "row", axis=1, tiled=True),
        matrix,
        (((1,), (1,)), ((), ())),
        preferred_element_type=jnp.float32,
    )


def local(start_vectors, cluster_order, weights, block_mask):
    row_index = lax.axis_index("row")
    col_index = lax.axis_index("col")
    row_count = lax.axis_size("row")
    col_count = lax.axis_size("col")
    block_len = start_vectors.shape[1]
    stored = weights[:, 0, :]
    live_mask = block_mask[:, 0, :]
    local_rows = row_index * col_count * block_len + jnp.arange(
        col_count * block_len, dtype=jnp.int32
    )
    col_position = jnp.arange(row_count * block_len, dtype=jnp.int32)
    local_cols = (
        col_position // block_len * col_count + col_index
    ) * block_len + col_position % block_len
    row_spans = row_index * col_count + jnp.arange(col_count, dtype=jnp.int32)
    col_spans = jnp.arange(row_count, dtype=jnp.int32) * col_count + col_index
    same_block = row_spans[:, None] == col_spans[None, :]
    keep_upper = ((live_mask > 0) | same_block)[:, None, :, None] & (
        local_rows.reshape(col_count, block_len, 1, 1)
        < local_cols.reshape(1, 1, row_count, block_len)
    )
    zero_value = jnp.zeros((), jnp.bfloat16)
    upper_part = jnp.where(
        keep_upper, stored.reshape(col_count, block_len, row_count, block_len), zero_value
    )
    ones_cols = jnp.ones((row_count * block_len,), jnp.bfloat16)
    matrix = upper_part.reshape(col_count * block_len, row_count * block_len)
    ones_rows = jnp.ones((col_count * block_len,), jnp.bfloat16)

    def mirror_sums(term):
        return lax.psum_scatter(term, "row", scatter_dimension=1, tiled=True)

    row_totals = jnp.dot(matrix, ones_cols, preferred_element_type=jnp.float32)[None, :]
    col_totals = jnp.dot(ones_rows, matrix, preferred_element_type=jnp.float32)[None, :]
    degree = collect_direct(row_totals) + mirror_sums(col_totals)
    inverse_root = 1.0 / jnp.sqrt(degree)
    picked = jnp.take_along_axis(
        start_vectors, jnp.broadcast_to(cluster_order, start_vectors.shape), axis=1
    )
    panel_now = orthonormalize(picked)
    for round_index in range(ITERS):
        vectors = (inverse_root * panel_now).astype(jnp.bfloat16)
        panel_now = orthonormalize(
            panel_now
            + inverse_root
            * (
                collect_direct(direct_part(matrix, vectors))
                + mirror_sums(
                    jnp.dot(
                        lax.all_gather(vectors, "col", axis=1, tiled=True),
                        matrix,
                        preferred_element_type=jnp.float32,
                    )
                )
            )
        )
    total_nodes = block_len * row_count * col_count
    return math.sqrt(total_nodes) * panel_now


def solution(mesh):
    placed = (
        P(None, ("row", "col")),
        P(("row", "col"), None),
        P("row", "col", None),
        P("row", "col", None),
    )
    return jax.shard_map(
        local, mesh=mesh, in_specs=placed, out_specs=P(None, ("row", "col")), check_vma=False
    )
```

profile of v0, /device:TPU:1, one launch (start us, length us, event | category | flops | bytes accessed | tf_op | source)
XLA Modules:
  0.0 1080.2 jit_solution(14854760492870772984)
XLA Ops:
  6.5 0.7 broadcast_compare_fusion
  7.3 0.1 bitcast_or_fusion
  7.4 1.1 and.66
  8.5 7.7 fusion
  16.3 3.2 copy-done.1
  19.5 3.4 convolution_bitcast_fusion.1
  23.0 7.7 convolution_bitcast_fusion
  30.9 50.7 %gather_fusion = f32[8192]{0:T(1024)S(1)} fusion(f32[64,128]{1,0:T(8,128)S(1)} %copy-done, s32[8192]{0:T(1024)S(1)} %or_bitcast_fusion), kind=kCustom, calls=%fused_computation | custom fusion | bytes 131072 | tf_op jit(solution)/shard_map/jit(take_along_axis)/gather | solution.py:73
  81.5 0.2 fusion.16
  81.7 82.8 %psum.28 = f32[64,64]{0,1:T(8,128)S(1)} all-reduce(f32[64,64]{0,1:T(8,128)S(1)} %fusion.16), channel_id=1, replica_groups=mesh['row'=16,'col'=16] {'row','col'}, use_global_device_ids=true, to_apply=%region_0.1 | all-reduce | flops 4096 | bytes 32768 | tf_op jit(solution)/shard_map/psum | solution.py:18
  164.6 0.1 copy.22
  164.7 5.8 cholesky.74
  170.5 0.6 compare_reduce_fusion.3
  171.2 0.7 fusion.1
  171.8 4.9 custom-call.10
  176.8 0.9 copy.34
  177.7 4.9 reduce-scatter.27.cloned.1.call-done
  182.5 0.9 copy.36
  183.4 0.3 multiply_convert_fusion.2
  183.7 32.5 %all_gather.18 = bf16[64,2048]{1,0:T(8,128)(2,1)S(1)} all-gather(bf16[64,128]{1,0:T(8,128)(2,1)S(1)} %get-tuple-element.6), channel_id=1, replica_groups=mesh['row'=16,'col'=16] {'row'}, dimensions={1}, use_global_device_ids=true | all-gather | bytes 278528 | tf_op jit(solution)/shard_map/all_gather | solution.py:29
  216.2 6.9 fusion.59
  223.1 50.3 %all_gather.19 = bf16[64,2048]{1,0:T(8,128)(2,1)S(1)} all-gather(bf16[64,128]{1,0:T(8,128)(2,1)S(1)} %get-tuple-element.6), channel_id=1, replica_groups=mesh['row'=16,'col'=16] {'col'}, dimensions={1}, use_global_device_ids=true | all-gather | bytes 278528 | tf_op jit(solution)/shard_map/all_gather | solution.py:86
  273.5 5.8 fusion.60
  279.4 35.2 %reduce-scatter.13.cloned.1.call-done = f32[64,128]{1,0:T(8,128)} async-done(((f32[64,2048]{1,0:T(8,128)}), f32[64,128]{1,0:T(8,128)}) %reduce-scatter.13.cloned.1.call-update) | async-done | bytes 32784 | tf_op jit(solution)/shard_map/reduce_scatter | solution.py:24
  314.6 75.0 %reduce-scatter.15.cloned.1.call-done = f32[64,128]{1,0:T(8,128)} async-done(((f32[64,2048]{1,0:T(8,128)}), f32[64,128]{1,0:T(8,128)}) %reduce-scatter.15.cloned.1.call-update) | async-done | bytes 32784 | tf_op jit(solution)/shard_map/reduce_scatter | solution.py:67
  389.6 0.8 multiply_add_fusion.2
  390.4 0.2 fusion.61
  390.6 85.2 %psum.29 = f32[64,64]{0,1:T(8,128)S(1)} all-reduce(f32[64,64]{0,1:T(8,128)S(1)} %fusion.61), channel_id=1, replica_groups=mesh['row'=16,'col'=16] {'row','col'}, use_global_device_ids=true, to_apply=%region_7.10 | all-reduce | flops 4096 | bytes 32768 | tf_op jit(solution)/shard_map/psum | solution.py:18
  475.7 0.1 copy.24
  475.8 5.8 cholesky.85
  481.7 0.6 compare_reduce_fusion.2
  482.3 0.7 fusion.2
  483.0 4.9 custom-call.11
  487.9 0.3 multiply_convert_fusion.1
  488.2 34.1 %all_gather.20 = bf16[64,2048]{1,0:T(8,128)(2,1)S(1)} all-gather(bf16[64,128]{1,0:T(8,128)(2,1)S(1)} %get-tuple-element.9), channel_id=1, replica_groups=mesh['row'=16,'col'=16] {'row'}, dimensions={1}, use_global_device_ids=true | all-gather | bytes 278528 | tf_op jit(solution)/shard_map/all_gather | solution.py:29
  522.3 6.9 fusion.62
  529.2 36.1 %all_gather.21 = bf16[64,2048]{1,0:T(8,128)(2,1)S(1)} all-gather(bf16[64,128]{1,0:T(8,128)(2,1)S(1)} %get-tuple-element.9), channel_id=1, replica_groups=mesh['row'=16,'col'=16] {'col'}, dimensions={1}, use_global_device_ids=true | all-gather | bytes 278528 | tf_op jit(solution)/shard_map/all_gather | solution.py:86
  565.3 5.8 fusion.63
  571.2 35.5 %reduce-scatter.17.cloned.1.call-done = f32[64,128]{1,0:T(8,128)} async-done(((f32[64,2048]{1,0:T(8,128)}), f32[64,128]{1,0:T(8,128)}) %reduce-scatter.17.cloned.1.call-update) | async-done | bytes 32784 | tf_op jit(solution)/shard_map/reduce_scatter | solution.py:24
  606.7 74.7 %reduce-scatter.19.cloned.1.call-done = f32[64,128]{1,0:T(8,128)} async-done(((f32[64,2048]{1,0:T(8,128)}), f32[64,128]{1,0:T(8,128)}) %reduce-scatter.19.cloned.1.call-update) | async-done | bytes 32784 | tf_op jit(solution)/shard_map/reduce_scatter | solution.py:67
  681.4 0.8 multiply_add_fusion.1
  682.2 0.2 fusion.64
  682.4 85.6 %psum.30 = f32[64,64]{0,1:T(8,128)S(1)} all-reduce(f32[64,64]{0,1:T(8,128)S(1)} %fusion.64), channel_id=1, replica_groups=mesh['row'=16,'col'=16] {'row','col'}, use_global_device_ids=true, to_apply=%region_10.13 | all-reduce | flops 4096 | bytes 32768 | tf_op jit(solution)/shard_map/psum | solution.py:18
  768.0 0.1 copy.26
  768.1 5.8 cholesky.96
  774.0 0.6 compare_reduce_fusion.1
  774.6 0.7 fusion.3
  775.3 4.9 custom-call.12
  780.2 0.3 multiply_convert_fusion
  780.4 34.1 %all_gather.22 = bf16[64,2048]{1,0:T(8,128)(2,1)S(1)} all-gather(bf16[64,128]{1,0:T(8,128)(2,1)S(1)} %get-tuple-element.11), channel_id=1, replica_groups=mesh['row'=16,'col'=16] {'row'}, dimensions={1}, use_global_device_ids=true | all-gather | bytes 278528 | tf_op jit(solution)/shard_map/all_gather | solution.py:29
  814.5 6.9 fusion.65
  821.5 35.9 %all_gather.23 = bf16[64,2048]{1,0:T(8,128)(2,1)S(1)} all-gather(bf16[64,128]{1,0:T(8,128)(2,1)S(1)} %get-tuple-element.11), channel_id=1, replica_groups=mesh['row'=16,'col'=16] {'col'}, dimensions={1}, use_global_device_ids=true | all-gather | bytes 278528 | tf_op jit(solution)/shard_map/all_gather | solution.py:86
  857.4 5.8 fusion.66
  863.2 35.7 %reduce-scatter.21.cloned.1.call-done = f32[64,128]{1,0:T(8,128)} async-done(((f32[64,2048]{1,0:T(8,128)}), f32[64,128]{1,0:T(8,128)}) %reduce-scatter.21.cloned.1.call-update) | async-done | bytes 32784 | tf_op jit(solution)/shard_map/reduce_scatter | solution.py:24
  899.0 75.8 %reduce-scatter.23.cloned.1.call-done = f32[64,128]{1,0:T(8,128)} async-done(((f32[64,2048]{1,0:T(8,128)}), f32[64,128]{1,0:T(8,128)}) %reduce-scatter.23.cloned.1.call-update) | async-done | bytes 32784 | tf_op jit(solution)/shard_map/reduce_scatter | solution.py:67
  974.7 0.8 multiply_add_fusion
  975.5 0.2 fusion.67
  975.7 84.6 %psum.31 = f32[64,64]{0,1:T(8,128)S(1)} all-reduce(f32[64,64]{0,1:T(8,128)S(1)} %fusion.67), channel_id=1, replica_groups=mesh['row'=16,'col'=16] {'row','col'}, use_global_device_ids=true, to_apply=%region_13.16 | all-reduce | flops 4096 | bytes 32768 | tf_op jit(solution)/shard_map/psum | solution.py:18
  1060.3 0.1 copy.28
  1060.4 5.8 cholesky.107
  1066.3 0.6 compare_reduce_fusion
  1066.9 0.7 fusion.4
  1067.6 4.9 custom-call.13
  1072.5 0.9 convolution_multiply_fusion
  (36 shorter events, 0.7 us)
Async XLA Ops:
  6.5 24.3 %copy-start = (f32[64,128]{1,0:T(8,128)S(1)}, f32[64,128]{1,0:T(8,128)}, u32[]{:S(2)}) copy-start(f32[64,128]{1,0:T(8,128)} %param.7) | copy-start | bytes 98308
  6.5 170.2 %reduce-scatter.25.cloned.1.call-start = ((), (), s32[]{:S(2)}) async-start(), calls=%async_computation.14 | async-start | bytes 1114112
  16.3 3.2 copy-start.1
  22.9 7.9 copy-start.2
  22.9 159.6 %reduce-scatter.27.cloned.1.call-start = ((), (), s32[]{:S(2)}) async-start(), calls=%async_computation.15 | async-start | bytes 1114112
  30.7 283.8 %reduce-scatter.13.cloned.1.call-start = ((), (), s32[]{:S(2)}) async-start(), calls=%async_computation.8 | async-start | bytes 557056 | tf_op jit(solution)/shard_map/reduce_scatter | solution.py:24
  223.1 166.5 %reduce-scatter.15.cloned.1.call-start = ((), (), s32[]{:S(2)}) async-start(), calls=%async_computation.9 | async-start | bytes 557056 | tf_op jit(solution)/shard_map/reduce_scatter | solution.py:67
  279.3 327.4 %reduce-scatter.17.cloned.1.call-start = ((), (), s32[]{:S(2)}) async-start(), calls=%async_computation.10 | async-start | bytes 557056 | tf_op jit(solution)/shard_map/reduce_scatter | solution.py:24
  529.2 152.2 %reduce-scatter.19.cloned.1.call-start = ((), (), s32[]{:S(2)}) async-start(), calls=%async_computation.11 | async-start | bytes 557056 | tf_op jit(solution)/shard_map/reduce_scatter | solution.py:67
  571.1 327.8 %reduce-scatter.21.cloned.1.call-start = ((), (), s32[]{:S(2)}) async-start(), calls=%async_computation.12 | async-start | bytes 557056 | tf_op jit(solution)/shard_map/reduce_scatter | solution.py:24
  821.4 153.3 %reduce-scatter.23.cloned.1.call-start = ((), (), s32[]{:S(2)}) async-start(), calls=%async_computation.13 | async-start | bytes 557056 | tf_op jit(solution)/shard_map/reduce_scatter | solution.py:67
Sparse Core Ops, SparseCore 0:
  23.1 81.6 reduce-scatter.24
  107.3 75.2 reduce-scatter.26
  223.2 91.2 reduce-scatter.12
  316.9 72.6 reduce-scatter.14
  529.3 77.3 reduce-scatter.16
  609.1 72.2 reduce-scatter.18
  821.5 77.3 reduce-scatter.20
  901.4 73.2 reduce-scatter.22
where the time goes:
time: 1080 us
  blocking collectives  561 us (52%)
  waiting for transfers between devices  337 us (31%)
  other arithmetic  59.2 us (5%)
  local copies, waits for them, and re-layouts  57.1 us (5%)
  matrix products  51.7 us (5%)
  between operations  13.8 us (1%)
    psum x4, blocking collectives, orthonormalize(): total_gram = lax.psum(partial_gram, ('row', 'col'))  338 us
    reduce_scatter x3, waiting for transfers between devices, mirror_sums(): return lax.psum_scatter(term, 'row', scatter_dimension=1, tiled=True)  225 us
    all_gather x3, blocking collectives, local(): lax.all_gather(vectors, 'col', axis=1, tiled=True)  122 us
    reduce_scatter x3, waiting for transfers between devices, collect_direct(): return lax.psum_scatter(term, 'col', scatter_dimension=1, tiled=True)  106 us
    all_gather x3, blocking collectives, direct_part(): lax.all_gather(vectors, 'row', axis=1, tiled=True)  101 us
    gather x1, local copies, waits for them, and re-layouts, local(): jnp.take_along_axis(start_vectors, jnp.broadcast_to(cluster_order, start_...  50.7 us
    another operation x12, other arithmetic, orthonormalize(): factor = jnp.linalg.cholesky(total_gram)  26.1 us
    another operation x8, other arithmetic, orthonormalize(): return jax.scipy.linalg.solve_triangular(factor, panel_in, lower=True)  22.2 us
  transfers between devices with their start and end apart: 8, of which 7 were waited for; matrix products, arithmetic and copies ran while one was open for 8% of the time, Pallas kernels for 0%

commit v1 on v0

--- a/solution.py
+++ b/solution.py
@@ -15,7 +15,7 @@
         precision=lax.Precision.HIGHEST,
         preferred_element_type=jnp.float32,
     )
-    total_gram = lax.psum(partial_gram, ("row", "col"))
+    total_gram = lax.psum(lax.psum(partial_gram, "row"), "col")
     factor = jnp.linalg.cholesky(total_gram)
     return jax.scipy.linalg.solve_triangular(factor, panel_in, lower=True)
 

time: 1080 us -> 1400 us (1.30)
  blocking collectives: 561 us -> 862 us
    psum x4 -> x8, blocking collectives: 338 us -> 647 us  [orthonormalize(): total_gram = lax.psum(lax.psum(partial_gram, 'row'), 'col')]
    reduce_scatter x3, waiting for transfers between devices: 106 us -> 121 us  [collect_direct(): return lax.psum_scatter(term, 'col', scatter_dimension=1, tiled=True)]
  transfers between devices with their start and end apart: 8 -> 8, of which waited for: 7 -> 6; matrix products, arithmetic and copies ran while one was open for 8% -> 6% of each run, Pallas kernels for 0% -> 0%
where the time goes in v1:
time: 1400 us; the launch traced here: 1390 us
  blocking collectives  862 us (62%)
  waiting for transfers between devices  348 us (25%)
  other arithmetic  59.2 us (4%)
  local copies, waits for them, and re-layouts  57.2 us (4%)
  matrix products  51.7 us (4%)
    psum x8, blocking collectives, orthonormalize(): total_gram = lax.psum(lax.psum(partial_gram, 'row'), 'col')  647 us
    reduce_scatter x3, waiting for transfers between devices, mirror_sums(): return lax.psum_scatter(term, 'row', scatter_dimension=1, tiled=True)  226 us
    reduce_scatter x3, waiting for transfers between devices, collect_direct(): return lax.psum_scatter(term, 'col', scatter_dimension=1, tiled=True)  121 us
    all_gather x3, blocking collectives, local(): lax.all_gather(vectors, 'col', axis=1, tiled=True)  119 us
    all_gather x3, blocking collectives, direct_part(): lax.all_gather(vectors, 'row', axis=1, tiled=True)  96.5 us
    gather x1, local copies, waits for them, and re-layouts, local(): jnp.take_along_axis(start_vectors, jnp.broadcast_to(cluster_order, start_...  50.7 us
  transfers between devices with their start and end apart: 8, of which 6 were waited for; matrix products, arithmetic and copies ran while one was open for 6% of the time, Pallas kernels for 0%

profile of v1, /device:TPU:1, one launch (start us, length us, event | category | flops | bytes accessed | tf_op | source)
XLA Modules:
  0.0 1392.0 jit_solution(7141730405209336479)
XLA Ops:
  6.5 0.7 broadcast_compare_fusion
  7.3 0.1 bitcast_or_fusion
  7.4 1.1 and.66
  8.5 7.7 fusion
  16.3 3.2 copy-done.1
  19.5 3.4 convolution_bitcast_fusion.1
  23.0 7.7 convolution_bitcast_fusion
  30.9 50.7 %gather_fusion = f32[8192]{0:T(1024)S(1)} fusion(f32[64,128]{1,0:T(8,128)S(1)} %copy-done, s32[8192]{0:T(1024)S(1)} %or_bitcast_fusion), kind=kCustom, calls=%fused_computation | custom fusion | bytes 131072 | tf_op jit(solution)/shard_map/jit(take_along_axis)/gather | solution.py:73
  81.5 0.2 fusion.16
  81.7 69.3 %psum.56 = f32[64,64]{0,1:T(8,128)S(1)} all-reduce(f32[64,64]{0,1:T(8,128)S(1)} %fusion.16), channel_id=1, replica_groups=mesh['row'=16,'col'=16] {'row'}, use_global_device_ids=true, to_apply=%region_0.1 | all-reduce | flops 4096 | bytes 32768 | tf_op jit(solution)/shard_map/psum | solution.py:18
  151.0 89.9 %psum.57 = f32[64,64]{0,1:T(8,128)S(1)} all-reduce(f32[64,64]{0,1:T(8,128)S(1)} %psum.56), channel_id=1, replica_groups=mesh['row'=16,'col'=16] {'col'}, use_global_device_ids=true, to_apply=%region_1.2 | all-reduce | flops 4096 | bytes 32768 | tf_op jit(solution)/shard_map/psum | solution.py:18
  241.0 0.1 copy.22
  241.1 5.8 cholesky.74
  246.9 0.6 compare_reduce_fusion.3
  247.6 0.7 fusion.1
  248.2 4.9 custom-call.10
  253.2 0.9 copy.34
  254.1 0.9 copy.36
  255.0 0.3 multiply_convert_fusion.2
  255.3 32.1 %all_gather.18 = bf16[64,2048]{1,0:T(8,128)(2,1)S(1)} all-gather(bf16[64,128]{1,0:T(8,128)(2,1)S(1)} %get-tuple-element.6), channel_id=1, replica_groups=mesh['row'=16,'col'=16] {'row'}, dimensions={1}, use_global_device_ids=true | all-gather | bytes 278528 | tf_op jit(solution)/shard_map/all_gather | solution.py:29
  287.4 6.9 fusion.59
  294.4 39.5 %all_gather.19 = bf16[64,2048]{1,0:T(8,128)(2,1)S(1)} all-gather(bf16[64,128]{1,0:T(8,128)(2,1)S(1)} %get-tuple-element.6), channel_id=1, replica_groups=mesh['row'=16,'col'=16] {'col'}, dimensions={1}, use_global_device_ids=true | all-gather | bytes 278528 | tf_op jit(solution)/shard_map/all_gather | solution.py:86
  333.9 5.8 fusion.60
  339.8 39.8 %reduce-scatter.13.cloned.1.call-done = f32[64,128]{1,0:T(8,128)} async-done(((f32[64,2048]{1,0:T(8,128)}), f32[64,128]{1,0:T(8,128)}) %reduce-scatter.13.cloned.1.call-update) | async-done | bytes 32784 | tf_op jit(solution)/shard_map/reduce_scatter | solution.py:24
  379.6 75.7 %reduce-scatter.15.cloned.1.call-done = f32[64,128]{1,0:T(8,128)} async-done(((f32[64,2048]{1,0:T(8,128)}), f32[64,128]{1,0:T(8,128)}) %reduce-scatter.15.cloned.1.call-update) | async-done | bytes 32784 | tf_op jit(solution)/shard_map/reduce_scatter | solution.py:67
  455.3 0.8 multiply_add_fusion.2
  456.1 0.2 fusion.61
  456.3 61.4 %psum.58 = f32[64,64]{0,1:T(8,128)S(1)} all-reduce(f32[64,64]{0,1:T(8,128)S(1)} %fusion.61), channel_id=1, replica_groups=mesh['row'=16,'col'=16] {'row'}, use_global_device_ids=true, to_apply=%region_8.11 | all-reduce | flops 4096 | bytes 32768 | tf_op jit(solution)/shard_map/psum | solution.py:18
  517.7 100.9 %psum.59 = f32[64,64]{0,1:T(8,128)S(1)} all-reduce(f32[64,64]{0,1:T(8,128)S(1)} %psum.58), channel_id=1, replica_groups=mesh['row'=16,'col'=16] {'col'}, use_global_device_ids=true, to_apply=%region_9.12 | all-reduce | flops 4096 | bytes 32768 | tf_op jit(solution)/shard_map/psum | solution.py:18
  618.7 5.8 cholesky.85
  624.6 0.6 compare_reduce_fusion.2
  625.2 0.7 fusion.2
  625.9 4.9 custom-call.11
  630.8 0.3 multiply_convert_fusion.1
  631.0 32.1 %all_gather.20 = bf16[64,2048]{1,0:T(8,128)(2,1)S(1)} all-gather(bf16[64,128]{1,0:T(8,128)(2,1)S(1)} %get-tuple-element.9), channel_id=1, replica_groups=mesh['row'=16,'col'=16] {'row'}, dimensions={1}, use_global_device_ids=true | all-gather | bytes 278528 | tf_op jit(solution)/shard_map/all_gather | solution.py:29
  663.1 6.9 fusion.62
  670.0 39.5 %all_gather.21 = bf16[64,2048]{1,0:T(8,128)(2,1)S(1)} all-gather(bf16[64,128]{1,0:T(8,128)(2,1)S(1)} %get-tuple-element.9), channel_id=1, replica_groups=mesh['row'=16,'col'=16] {'col'}, dimensions={1}, use_global_device_ids=true | all-gather | bytes 278528 | tf_op jit(solution)/shard_map/all_gather | solution.py:86
  709.5 5.8 fusion.63
  715.5 40.6 %reduce-scatter.17.cloned.1.call-done = f32[64,128]{1,0:T(8,128)} async-done(((f32[64,2048]{1,0:T(8,128)}), f32[64,128]{1,0:T(8,128)}) %reduce-scatter.17.cloned.1.call-update) | async-done | bytes 32784 | tf_op jit(solution)/shard_map/reduce_scatter | solution.py:24
  756.1 75.0 %reduce-scatter.19.cloned.1.call-done = f32[64,128]{1,0:T(8,128)} async-done(((f32[64,2048]{1,0:T(8,128)}), f32[64,128]{1,0:T(8,128)}) %reduce-scatter.19.cloned.1.call-update) | async-done | bytes 32784 | tf_op jit(solution)/shard_map/reduce_scatter | solution.py:67
  831.1 0.8 multiply_add_fusion.1
  831.8 0.2 fusion.64
  832.0 61.6 %psum.60 = f32[64,64]{0,1:T(8,128)S(1)} all-reduce(f32[64,64]{0,1:T(8,128)S(1)} %fusion.64), channel_id=1, replica_groups=mesh['row'=16,'col'=16] {'row'}, use_global_device_ids=true, to_apply=%region_12.15 | all-reduce | flops 4096 | bytes 32768 | tf_op jit(solution)/shard_map/psum | solution.py:18
  893.6 101.3 %psum.61 = f32[64,64]{0,1:T(8,128)S(1)} all-reduce(f32[64,64]{0,1:T(8,128)S(1)} %psum.60), channel_id=1, replica_groups=mesh['row'=16,'col'=16] {'col'}, use_global_device_ids=true, to_apply=%region_13.16 | all-reduce | flops 4096 | bytes 32768 | tf_op jit(solution)/shard_map/psum | solution.py:18
  995.0 5.8 cholesky.96
  1000.9 0.6 compare_reduce_fusion.1
  1001.5 0.7 fusion.3
  1002.2 4.9 custom-call.12
  1007.1 0.3 multiply_convert_fusion
  1007.4 32.3 %all_gather.22 = bf16[64,2048]{1,0:T(8,128)(2,1)S(1)} all-gather(bf16[64,128]{1,0:T(8,128)(2,1)S(1)} %get-tuple-element.11), channel_id=1, replica_groups=mesh['row'=16,'col'=16] {'row'}, dimensions={1}, use_global_device_ids=true | all-gather | bytes 278528 | tf_op jit(solution)/shard_map/all_gather | solution.py:29
  1039.6 6.9 fusion.65
  1046.6 39.7 %all_gather.23 = bf16[64,2048]{1,0:T(8,128)(2,1)S(1)} all-gather(bf16[64,128]{1,0:T(8,128)(2,1)S(1)} %get-tuple-element.11), channel_id=1, replica_groups=mesh['row'=16,'col'=16] {'col'}, dimensions={1}, use_global_device_ids=true | all-gather | bytes 278528 | tf_op jit(solution)/shard_map/all_gather | solution.py:86
  1086.3 5.8 fusion.66
  1092.1 40.8 %reduce-scatter.21.cloned.1.call-done = f32[64,128]{1,0:T(8,128)} async-done(((f32[64,2048]{1,0:T(8,128)}), f32[64,128]{1,0:T(8,128)}) %reduce-scatter.21.cloned.1.call-update) | async-done | bytes 32784 | tf_op jit(solution)/shard_map/reduce_scatter | solution.py:24
  1133.0 75.7 %reduce-scatter.23.cloned.1.call-done = f32[64,128]{1,0:T(8,128)} async-done(((f32[64,2048]{1,0:T(8,128)}), f32[64,128]{1,0:T(8,128)}) %reduce-scatter.23.cloned.1.call-update) | async-done | bytes 32784 | tf_op jit(solution)/shard_map/reduce_scatter | solution.py:67
  1208.7 0.8 multiply_add_fusion
  1209.5 0.2 fusion.67
  1209.7 60.9 %psum.62 = f32[64,64]{0,1:T(8,128)S(1)} all-reduce(f32[64,64]{0,1:T(8,128)S(1)} %fusion.67), channel_id=1, replica_groups=mesh['row'=16,'col'=16] {'row'}, use_global_device_ids=true, to_apply=%region_16.19 | all-reduce | flops 4096 | bytes 32768 | tf_op jit(solution)/shard_map/psum | solution.py:18
  1270.6 101.5 %psum.63 = f32[64,64]{0,1:T(8,128)S(1)} all-reduce(f32[64,64]{0,1:T(8,128)S(1)} %psum.62), channel_id=1, replica_groups=mesh['row'=16,'col'=16] {'col'}, use_global_device_ids=true, to_apply=%region_17.20 | all-reduce | flops 4096 | bytes 32768 | tf_op jit(solution)/shard_map/psum | solution.py:18
  1372.2 5.8 cholesky.107
  1378.0 0.6 compare_reduce_fusion
  1378.7 0.7 fusion.4
  1379.3 4.9 custom-call.13
  1384.2 0.9 convolution_multiply_fusion
  (40 shorter events, 0.9 us)
Async XLA Ops:
  6.5 24.3 %copy-start = (f32[64,128]{1,0:T(8,128)S(1)}, f32[64,128]{1,0:T(8,128)}, u32[]{:S(2)}) copy-start(f32[64,128]{1,0:T(8,128)} %param.7) | copy-start | bytes 98308
  6.5 246.6 %reduce-scatter.25.cloned.1.call-start = ((), (), s32[]{:S(2)}) async-start(), calls=%async_computation.14 | async-start | bytes 1114112
  16.3 3.2 copy-start.1
  22.9 7.9 copy-start.2
  22.9 231.1 %reduce-scatter.27.cloned.1.call-start = ((), (), s32[]{:S(2)}) async-start(), calls=%async_computation.15 | async-start | bytes 1114112
  30.7 348.9 %reduce-scatter.13.cloned.1.call-start = ((), (), s32[]{:S(2)}) async-start(), calls=%async_computation.8 | async-start | bytes 557056 | tf_op jit(solution)/shard_map/reduce_scatter | solution.py:24
  294.3 161.0 %reduce-scatter.15.cloned.1.call-start = ((), (), s32[]{:S(2)}) async-start(), calls=%async_computation.9 | async-start | bytes 557056 | tf_op jit(solution)/shard_map/reduce_scatter | solution.py:67
  339.8 416.3 %reduce-scatter.17.cloned.1.call-start = ((), (), s32[]{:S(2)}) async-start(), calls=%async_computation.10 | async-start | bytes 557056 | tf_op jit(solution)/shard_map/reduce_scatter | solution.py:24
  670.0 161.1 %reduce-scatter.19.cloned.1.call-start = ((), (), s32[]{:S(2)}) async-start(), calls=%async_computation.11 | async-start | bytes 557056 | tf_op jit(solution)/shard_map/reduce_scatter | solution.py:67
  715.4 417.6 %reduce-scatter.21.cloned.1.call-start = ((), (), s32[]{:S(2)}) async-start(), calls=%async_computation.12 | async-start | bytes 557056 | tf_op jit(solution)/shard_map/reduce_scatter | solution.py:24
  1046.6 162.1 %reduce-scatter.23.cloned.1.call-start = ((), (), s32[]{:S(2)}) async-start(), calls=%async_computation.13 | async-start | bytes 557056 | tf_op jit(solution)/shard_map/reduce_scatter | solution.py:67
Sparse Core Ops, SparseCore 0:
  23.1 81.7 reduce-scatter.24
  107.3 74.5 reduce-scatter.26
  294.5 85.1 reduce-scatter.12
  382.0 73.2 reduce-scatter.14
  670.1 85.9 reduce-scatter.16
  758.4 72.5 reduce-scatter.18
  1046.7 86.2 reduce-scatter.20
  1135.5 73.1 reduce-scatter.22
